TPU v7x, 256 devices: a whole 4x4x8 slice. The times are simulated.
256 devices in a mesh: group: 8 (over z), ghost: 32 (over x, y, core).
Axes of the slice: x: 4, y: 4, z: 8, core: 2. Of those that a mesh axis runs over, the one named last changes fastest.
Arguments:
- inputs: bfloat16 [200704, 1024], P(('group', 'ghost')), may hold values from -24 to 24
- out_grad: bfloat16 [200704, 1024], P(('group', 'ghost')), may hold values from -6 to 6
- conv_first: bfloat16 [1024, 256], replicated, may hold values from -0.25 to 0.25
- conv_middle: bfloat16 [2304, 256], replicated, may hold values from -0.1875 to 0.1875
- conv_last: bfloat16 [256, 1024], replicated, may hold values from -0.375 to 0.375
- gain: float32 [1024], replicated, may hold values from 0.5 to 1.5
Outputs:
- input_grad: bfloat16 [200704, 1024], P(('group', 'ghost'))
- first_grad: float32 [262144], P(('group', 'ghost'))
- middle_grad: float32 [589824], P(('group', 'ghost'))
- last_grad: float32 [262144], P(('group', 'ghost'))
- gain_grad: float32 [1024], P(('group', 'ghost'))
All inputs are finite; a program needn't handle non-finite values.
Results may differ from a plain program's by a relative error of at most 0.0071.
Values sent between devices are 32-bit elements; how exact they have to be, the bound alone decides.
A program may use at most 128 MiB of HBM per device.

v0:
```python
import jax
import jax.numpy as jnp
from jax import lax
from jax.experimental import pallas as pl
from jax.experimental.pallas import tpu as pltpu
from jax.sharding import PartitionSpec as P

GROUP = 64
NEWTON = 5
SIDE = 14
PAD = 16
TILE = 112
MESH = pl.DeviceIdType.MESH
epsilon = 1e-05
F32 = jnp.float32
BF16 = jnp.bfloat16


def dot(left, right, dims=((1,), (0,))):
    return lax.dot_general(left, right, (dims, ((), ())), preferred_element_type=F32)


def parts(value, count):
    pieces = []
    for _ in range(count):
        piece = value.astype(BF16)
        pieces.append(piece)
        value = value - piece.astype(F32)
    return pieces


def dot_parts(left, right, dims=((1,), (0,))):
    total = None
    for a in left:
        for b in right:
            term = dot(a, b, dims)
            total = term if total is None else total + term
    return total


def dot_high(left, right, dims=((1,), (0,))):
    return lax.dot_general(
        left, right, (dims, ((), ())), preferred_element_type=F32, precision=lax.Precision.HIGHEST
    )


def tile_rows(t):
    return pl.ds(pl.multiple_of(t * TILE, TILE), TILE)


def fold(block, right):
    top, low = block[:32], block[32:]
    lane = lax.broadcasted_iota(jnp.int32, (32, 128), 1)
    if right:
        top = pltpu.roll(top, 64, 1)
    else:
        low = pltpu.roll(low, 64, 1)
    return jnp.where(lane < 64, top, low)


def unfold(folded, right):
    lane = lax.broadcasted_iota(jnp.int32, (32, 128), 1)
    other = pltpu.roll(folded, 64, 1)
    top, low = (other, folded) if right else (folded, other)
    keep = (lane >= 64) if right else (lane < 64)
    return jnp.where(keep, top, 0.0), jnp.where(keep, low, 0.0)


def fill_diagonal(target, source):
    target[...] = jnp.zeros_like(target)
    for k in range(16):
        j, at = k // 4, (k % 4) * GROUP
        lanes = slice((at // 128) * 128, (at // 128) * 128 + 128)
        top, low = unfold(source[k, :32, :], bool(k % 2))
        target[j, at : at + 32, lanes] = top
        target[j, at + 32 : at + 64, lanes] = low


def fill_row(target, source):
    lane = lax.broadcasted_iota(jnp.int32, (8, 128), 1)
    for pair in range(8):
        left = source[2 * pair, 32:40, :]
        right = pltpu.roll(source[2 * pair + 1, 32:40, :], 64, 1)
        target[:, pair * 128 : pair * 128 + 128] = jnp.where(lane < 64, left, right)


def pack_row(row, k):
    piece = row[:, (k // 2) * 128 : (k // 2) * 128 + 128]
    return pltpu.roll(piece, 64, 1) if k % 2 else piece


def edges(t):
    row = lax.broadcasted_iota(jnp.int32, (TILE, 256), 0).astype(F32) + float(t * TILE)
    line = jnp.floor((row + 0.5) * (1.0 / SIDE))
    column = row - line * SIDE
    image = jnp.floor((line + 0.5) * (1.0 / SIDE))
    return line - image * SIDE, column


def shifted_tiles(padded, columns, sign):
    for t in range(columns.shape[0] // TILE):
        line, column = edges(t)
        at = slice(t * TILE, t * TILE + TILE)
        for tap in range(9):
            dr, dc = sign * (tap // 3 - 1), sign * (tap % 3 - 1)
            start = t * TILE + PAD + dr * SIDE + dc
            value = padded[start : start + TILE, :]
            keep = None
            if dr:
                keep = line > 0.5 if dr < 0 else line < SIDE - 1.5
            if dc:
                side = column > 0.5 if dc < 0 else column < SIDE - 1.5
                keep = side if keep is None else keep & side
            if keep is not None:
                value = jnp.where(keep, value, 0.0)
            columns[at, tap * 256 : tap * 256 + 256] = value.astype(BF16)


def forward_kernel(x, a, b, c, h1, s1, h2, s2, gram, hsum, payload, acc, padded, columns, wide):
    rows = x.shape[0]
    acc[...] = dot(x[...], a[...])
    padded[:PAD, :] = jnp.zeros((PAD, 256), F32)
    padded[rows + PAD :, :] = jnp.zeros((PAD, 256), F32)

    def first(t, carry):
        v = acc[tile_rows(t), :]
        s = 1.0 / (1.0 + jnp.exp(-v))
        s1[tile_rows(t), :] = s * (1.0 + v * (1.0 - s))
        h = (v * s).astype(BF16)
        h1[tile_rows(t), :] = h
        padded[pl.ds(t * TILE + PAD, TILE), :] = h.astype(F32)
        return carry

    lax.fori_loop(0, rows // TILE, first, 0)
    shifted_tiles(padded, columns, 1)
    acc[...] = dot(columns[...], b[...])

    def second(t, carry):
        v = acc[tile_rows(t), :]
        s = 1.0 / (1.0 + jnp.exp(-v))
        s2[tile_rows(t), :] = s * (1.0 + v * (1.0 - s))
        h2[tile_rows(t), :] = (v * s).astype(BF16)
        return carry

    lax.fori_loop(0, rows // TILE, second, 0)
    h = h2[...]
    gram[...] = dot(h, h, ((0,), (0,)))
    hsum[...] = dot(h, jnp.ones((rows, 128), BF16), ((0,), (0,)))
    wide[...] = dot_parts(parts(gram[...], 3), [c[...]])
    row = dot(jnp.ones((8, rows), BF16), h)
    brow = dot_parts(parts(row, 3), [c[...]])
    for j in range(4):
        here = slice(j * 256, j * 256 + 256)
        square = dot_parts([c[:, here]], parts(wide[:, here], 3), ((0,), (0,)))
        for q in range(4):
            k = 4 * j + q
            lanes = slice((q // 2) * 128, (q // 2) * 128 + 128)
            payload[k, :32, :] = fold(square[q * 64 : q * 64 + 64, lanes], bool(q % 2))
            payload[k, 32:40, :] = pack_row(brow, k)


def middle_kernel(whites, h2, x, og, gain, c, dpre, dwhite, d, across, gains, payload, diagonal, offset, white, csum):
    rows = x.shape[0]
    fill_diagonal(diagonal, whites)
    fill_row(offset, whites)
    for j in range(4):
        here = slice(j * 256, j * 256 + 256)
        folded = dot_parts([c[:, here]], parts(diagonal[j], 2))
        high, low = parts(folded, 2)
        d[:, here] = high
        white[:, here] = dot(h2[...], high) + dot(h2[...], low)
    csum[...] = jnp.zeros_like(csum)
    gains[...] = jnp.zeros_like(gains)

    def body(t, carry):
        for j in range(8):
            here = slice(j * 128, j * 128 + 128)
            w = white[tile_rows(t), here] - offset[0:1, here]
            g = gain[0:1, here]
            v = x[tile_rows(t), here].astype(F32) + g * w
            s = 1.0 / (1.0 + jnp.exp(-v))
            u = og[tile_rows(t), here].astype(F32) * (s * (1.0 + v * (1.0 - s)))
            dpre[tile_rows(t), here] = u
            dw = g * u
            dwhite[tile_rows(t), here] = dw.astype(BF16)
            csum[:, here] += jnp.sum(dw.reshape(TILE // 8, 8, 128), axis=0)
            gains[:, here] += jnp.sum((u * w).reshape(TILE // 8, 8, 128), axis=0)
        return carry

    lax.fori_loop(0, rows // TILE, body, 0)
    across[...] = dot(h2[...], dwhite[...], ((0,), (0,)))
    total = jnp.broadcast_to(jnp.sum(csum[...], axis=0, keepdims=True), (8, csum.shape[1]))
    for j in range(4):
        here = slice(j * 256, j * 256 + 256)
        square = dot_parts([c[:, here]], parts(across[:, here], 2), ((0,), (0,)))
        for q in range(4):
            k = 4 * j + q
            lanes = slice((q // 2) * 128, (q // 2) * 128 + 128)
            payload[k, :32, :] = fold(square[q * 64 : q * 64 + 64, lanes], bool(q % 2))
            payload[k, 32:40, :] = pack_row(total, k)


def backward_kernel(
    span, slopes, whites, x, a, b, c, h1, s1, h2, s2, gram, hsum, dpre, dwhite, d, across, gains,
    input_grad, grads, acc, padded, columns, diagonal, e, last, mid, top, row,
):
    rows = x.shape[0]
    fill_diagonal(diagonal, slopes)
    fill_row(row, slopes)
    for j in range(4):
        here = slice(j * 256, j * 256 + 256)
        e[:, here] = (dot_parts([c[:, here]], parts(diagonal[j], 2)) * (1.0 / span)).astype(BF16)
    back = dot(e[...], c[...], ((1,), (1,))).astype(BF16)
    const = dot_parts(parts(row[...], 2), [c[...]], ((1,), (1,)))
    acc[...] = dot(dwhite[...], d[...], ((1,), (1,))) + dot(h2[...], back)
    padded[:PAD, :] = jnp.zeros((PAD, 256), F32)
    padded[rows + PAD :, :] = jnp.zeros((PAD, 256), F32)

    def second(t, carry):
        v = (acc[tile_rows(t), :] - const[0:1, :]) * s2[tile_rows(t), :]
        padded[pl.ds(t * TILE + PAD, TILE), :] = v.astype(BF16).astype(F32)
        return carry

    lax.fori_loop(0, rows // TILE, second, 0)
    shifted_tiles(padded, columns, -1)
    for tap in range(9):
        here = slice(tap * 256, tap * 256 + 256)
        term = dot(columns[:, here], b[here, :], ((1,), (1,)))
        if tap == 0:
            acc[...] = term
        else:
            acc[...] += term
        value = dot(h1[...], columns[:, here], ((0,), (0,)))
        for half in range(2):
            mid[half, here, :] = value[:, half * 128 : half * 128 + 128]

    def first(t, carry):
        padded[pl.ds(t * TILE + PAD, TILE), :] = acc[tile_rows(t), :] * s1[tile_rows(t), :]
        return carry

    lax.fori_loop(0, rows // TILE, first, 0)
    dmid1 = padded[PAD : rows + PAD, :].astype(BF16)
    value = dot(x[...], dmid1, ((0,), (0,)))
    for half in range(2):
        top[half] = value[:, half * 128 : half * 128 + 128]
    for j in range(4):
        here = slice(j * 256, j * 256 + 256)
        input_grad[:, here] = (dot(dmid1, a[here, :], ((1,), (1,))) + dpre[:, here]).astype(BF16)
    fill_diagonal(diagonal, whites)
    grams = parts(gram[...], 2)
    for j in range(4):
        here = slice(j * 256, j * 256 + 256)
        high, low = parts(across[:, here], 2)
        white = parts(diagonal[j], 2)
        value = dot_parts([high], white, ((1,), (1,))) + dot(low, white[0], ((1,), (1,)))
        last[:, here] = value + dot_parts(grams, [e[:, here]])
    for j in range(8):
        here = slice(j * 128, j * 128 + 128)
        grads[:, 3328 + j * 128 : 3456 + j * 128] = last[:, here] - hsum[...] * row[0:1, here]
    for half in range(2):
        for q in range(4):
            at = q * 256 + half * 128
            grads[:, at : at + 128] = top[half, pl.ds(q, 256, stride=4), :]
        for q in range(9):
            at = 1024 + q * 256 + half * 128
            grads[:, at : at + 128] = mid[half, pl.ds(q, 256, stride=9), :]
    total = jnp.sum(gains[...], axis=0, keepdims=True)
    own = lax.broadcasted_iota(jnp.int32, (256, 1024), 0)
    channel = lax.broadcasted_iota(jnp.int32, (256, 1024), 1)
    spread = jnp.where((channel >> 2) == own, total, 0.0)
    channel = lax.broadcasted_iota(jnp.int32, (1024, 128), 0)
    lane = lax.broadcasted_iota(jnp.int32, (1024, 128), 1)
    pick = jnp.where((channel & 3) == lane, 1.0, 0.0).astype(BF16)
    grads[:, 4352:4480] = dot_parts(parts(spread, 3), [pick])


def newton(n, size):
    row = lax.broadcasted_iota(jnp.int32, (size, size), 0)
    lane = lax.broadcasted_iota(jnp.int32, (size, size), 1)
    project = jnp.where(row == lane, 1.5, 0.0) - 0.5 * n
    for sweep in range(NEWTON - 1):
        squared = dot_high(project, project)
        project = 1.5 * project - 0.5 * dot_high(squared, dot_high(project, n))
    return project


def trace_of(block, size=64):
    row = lax.broadcasted_iota(jnp.int32, (size, size), 0)
    lane = lax.broadcasted_iota(jnp.int32, (size, size), 1)
    return jnp.sum(jnp.where(row == lane, block, 0.0))


def square_of(folded):
    return jnp.concatenate([folded[:32, :64], pltpu.roll(folded[:32], 64, 1)[:, :64]], axis=0)


def folded_of(square):
    return jnp.concatenate([square[:32], square[32:]], axis=1)


def whiten_block(total, span):
    row64 = total[32:40, :64] * (1.0 / span)
    outer = dot_high(jnp.where(lax.broadcasted_iota(jnp.int32, (8, 64), 0) == 0, row64, 0.0), row64, ((0,), (0,)))
    r = lax.broadcasted_iota(jnp.int32, (64, 64), 0)
    c = lax.broadcasted_iota(jnp.int32, (64, 64), 1)
    cov = square_of(total) * (1.0 / span) - outer + jnp.where(r == c, epsilon, 0.0)
    trace = trace_of(cov)
    scaled = cov / trace
    white = newton(scaled, 64) / jnp.sqrt(jnp.full((64, 64), trace))
    offset = dot_high(row64, white)
    return cov, white, row64, offset


def slope_block(total, cov, white, mean, span):
    csum = total[32:40, :64]
    outer = dot_high(jnp.where(lax.broadcasted_iota(jnp.int32, (8, 64), 0) == 0, mean, 0.0), csum, ((0,), (0,)))
    cross = square_of(total) - outer
    trace = trace_of(cov)
    root = jnp.sqrt(jnp.full((64, 64), trace))
    scaled = cov / trace
    up = jnp.concatenate([scaled, cross / root], axis=1)
    low = jnp.concatenate([jnp.zeros((64, 64), F32), scaled], axis=1)
    project = newton(jnp.concatenate([up, low], axis=0), 128)
    dn = project[:64, 64:]
    dt = -jnp.sum(dn * scaled) / trace - 0.5 * jnp.sum(cross * white) / trace
    r = lax.broadcasted_iota(jnp.int32, (64, 64), 0)
    c = lax.broadcasted_iota(jnp.int32, (64, 64), 1)
    dcov = dn / trace + jnp.where(r == c, dt, 0.0)
    sym = dcov + dcov.T
    line = (dot_high(csum, white, ((1,), (1,))) + dot_high(mean, sym)) * (1.0 / span)
    return sym, line


def ghost_device(group, chip, core):
    return (group, chip * 2 + core)


def exchange_kernel(solve, payload, state, out, keep, got, part, other, mine, sems):
    group, ghost = lax.axis_index("group"), lax.axis_index("ghost")
    chip, core = ghost // 2, ghost % 2
    send, recv, send_back, recv_back, pair = sems
    barrier = pltpu.get_barrier_semaphore()

    def greet(s, carry):
        peer = ghost_device(group, (chip + s) % 16, core)
        pl.semaphore_signal(barrier, inc=1, device_id=peer, device_id_type=MESH)
        return carry

    lax.fori_loop(1, 16, greet, 0)
    partner = ghost_device(group, chip, 1 - core)
    pl.semaphore_signal(barrier, inc=1, device_id=partner, device_id_type=MESH)
    pl.semaphore_wait(barrier, 16)

    def scatter(s):
        target = (chip + s) % 16
        return pltpu.make_async_remote_copy(
            src_ref=payload.at[target], dst_ref=got.at[s], send_sem=send.at[s], recv_sem=recv.at[s],
            device_id=ghost_device(group, target, core), device_id_type=MESH,
        )

    def start(s, carry):
        scatter(s).start()
        return carry

    lax.fori_loop(1, 16, start, 0)
    part[...] = payload[chip]

    def add(s, carry):
        scatter(s).wait_recv()
        part[...] += got[s]
        return carry

    lax.fori_loop(1, 16, add, 0)
    swap = pltpu.make_async_remote_copy(
        src_ref=part, dst_ref=other, send_sem=pair.at[0], recv_sem=pair.at[1],
        device_id=partner, device_id_type=MESH,
    )
    swap.start()
    swap.wait_recv()
    solve(part[...] + other[...], state, mine, keep)
    out[chip] = mine[...]

    def spread(s):
        return pltpu.make_async_remote_copy(
            src_ref=mine, dst_ref=out.at[chip], send_sem=send_back.at[s], recv_sem=recv_back.at[s],
            device_id=ghost_device(group, (chip + s) % 16, core), device_id_type=MESH,
        )

    def arrival(s):
        return pltpu.make_async_remote_copy(
            src_ref=mine, dst_ref=out.at[(chip + 16 - s) % 16], send_sem=send_back.at[s],
            recv_sem=recv_back.at[s], device_id=ghost_device(group, (chip + s) % 16, core), device_id_type=MESH,
        )

    def start_back(s, carry):
        spread(s).start()
        return carry

    lax.fori_loop(1, 16, start_back, 0)

    def finish(s, carry):
        arrival(s).wait_recv()
        return carry

    lax.fori_loop(1, 16, finish, 0)

    def drain(s, carry):
        scatter(s).wait_send()
        spread(s).wait_send()
        return carry

    lax.fori_loop(1, 16, drain, 0)
    swap.wait_send()


def solve_white(span, total, state, mine, keep):
    cov, white, mean, offset = whiten_block(total, span)
    keep[:64] = cov
    keep[64:128] = white
    keep[128:136] = mean
    mine[:32, :] = folded_of(white)
    mine[32:40, :] = jnp.concatenate([offset, offset], axis=1)


def solve_slope(span, total, state, mine, keep):
    sym, line = slope_block(total, state[:64], state[64:128], state[128:136], span)
    keep[...] = jnp.zeros_like(keep)
    mine[:32, :] = folded_of(sym)
    mine[32:40, :] = jnp.concatenate([line, line], axis=1)


VM = pl.BlockSpec(memory_space=pltpu.VMEM)
LIMIT = pltpu.CompilerParams(vmem_limit_bytes=60 * 1024 * 1024)


def shape(dims, kind=F32):
    return jax.ShapeDtypeStruct(dims, kind)


def exchange(payload, state, span, solve, number, name):
    def body(payload, state, out, keep, got, part, other, mine, *sems):
        exchange_kernel(
            lambda *args: solve(span, *args), payload, state, out, keep, got, part, other, mine, sems
        )

    dma = pltpu.SemaphoreType.DMA
    return pl.pallas_call(
        body,
        out_shape=(shape((16, 40, 128)), shape((136, 64))),
        in_specs=[VM] * 2,
        out_specs=[VM] * 2,
        scratch_shapes=[
            pltpu.VMEM((16, 40, 128), F32),
            pltpu.VMEM((40, 128), F32),
            pltpu.VMEM((40, 128), F32),
            pltpu.VMEM((40, 128), F32),
            dma((16,)), dma((16,)), dma((16,)), dma((16,)), dma((2,)),
        ],
        compiler_params=pltpu.CompilerParams(collective_id=number, has_side_effects=True),
        name=name,
    )(payload, state)


def forward(x, a, b, c):
    rows = x.shape[0]
    return pl.pallas_call(
        forward_kernel,
        out_shape=(
            shape((rows, 256), BF16), shape((rows, 256)), shape((rows, 256), BF16), shape((rows, 256)),
            shape((256, 256)), shape((256, 128)), shape((16, 40, 128)),
        ),
        in_specs=[VM] * 4,
        out_specs=[VM] * 7,
        scratch_shapes=[
            pltpu.VMEM((rows, 256), F32),
            pltpu.VMEM((rows + 2 * PAD, 256), F32),
            pltpu.VMEM((rows, 2304), BF16),
            pltpu.VMEM((256, 1024), F32),
        ],
        compiler_params=LIMIT,
        name="forward",
    )(x, a, b, c)


def middle(whites, h2, x, og, gain, c):
    rows = x.shape[0]
    return pl.pallas_call(
        middle_kernel,
        out_shape=(
            shape((rows, 1024)), shape((rows, 1024), BF16), shape((256, 1024), BF16), shape((256, 1024)),
            shape((8, 1024)), shape((16, 40, 128)),
        ),
        in_specs=[VM] * 6,
        out_specs=[VM] * 6,
        scratch_shapes=[
            pltpu.VMEM((4, 256, 256), F32),
            pltpu.VMEM((8, 1024), F32),
            pltpu.VMEM((rows, 1024), F32),
            pltpu.VMEM((8, 1024), F32),
        ],
        compiler_params=LIMIT,
        name="middle",
    )(whites, h2, x, og, gain, c)


def backward(span, *args):
    rows = args[2].shape[0]

    def body(*refs):
        backward_kernel(span, *refs)

    return pl.pallas_call(
        body,
        out_shape=(shape((rows, 1024), BF16), shape((256, 4480))),
        in_specs=[VM] * len(args),
        out_specs=[VM] * 2,
        scratch_shapes=[
            pltpu.VMEM((rows, 256), F32),
            pltpu.VMEM((rows + 2 * PAD, 256), F32),
            pltpu.VMEM((rows, 2304), BF16),
            pltpu.VMEM((4, 256, 256), F32),
            pltpu.VMEM((256, 1024), BF16),
            pltpu.VMEM((256, 1024), F32),
            pltpu.VMEM((2, 2304, 128), F32),
            pltpu.VMEM((2, 1024, 128), F32),
            pltpu.VMEM((8, 1024), F32),
        ],
        compiler_params=LIMIT,
        name="backward",
    )(*args)


def shards(inputs, out_grad, conv_first, conv_middle, conv_last, gain):
    ghosts, groups = lax.axis_size("ghost"), lax.axis_size("group")
    span = float(inputs.shape[0] * ghosts)
    h1, s1, h2, s2, gram, hsum, payload = forward(inputs, conv_first, conv_middle, conv_last)
    whites, state = exchange(payload, jnp.zeros((136, 64), F32), span, solve_white, 0, "whiten")
    dpre, dwhite, d, across, gains, payload = middle(
        whites, h2, inputs, out_grad, gain.reshape(1, -1), conv_last
    )
    slopes, _ = exchange(payload, state, span, solve_slope, 1, "slope")
    input_grad, grads = backward(
        span, slopes, whites, inputs, conv_first, conv_middle, conv_last, h1, s1, h2, s2, gram, hsum,
        dpre, dwhite, d, across, gains,
    )
    grads = lax.psum_scatter(grads, ("group", "ghost"), scatter_dimension=0, tiled=True)
    grads = grads.reshape(-1) * (span * groups) ** (-0.5)
    return input_grad, grads[:1024], grads[1024:3328], grads[3328:4352], grads[4352:4356]


def solution(mesh):
    rows = P(("group", "ghost"))
    return jax.shard_map(
        shards,
        mesh=mesh,
        in_specs=(P(("group", "ghost"), None), P(("group", "ghost"), None), P(), P(), P(), P()),
        out_specs=(P(("group", "ghost"), None), rows, rows, rows, rows),
        check_vma=False,
    )
```

profile of v0, /device:TPU:2, one launch (start us, length us, event | category | flops | bytes accessed | tf_op | source)
XLA Modules:
  0.0 370.1 jit_solution(3293504693540297193)
XLA Ops:
  7.2 0.0 all-reduce.3.cloned.1.call-start
  7.2 8.6 %forward.1 = (bf16[784,256]{1,0:T(8,128)(2,1)}, f32[784,256]{1,0:T(8,128)}, bf16[784,256]{1,0:T(8,128)(2,1)}, f32[784,256]{1,0:T(8,128)}, f32[256,256]{1,0:T(8,1...) custom-call(bf16[784,1024]{1,0:T(8,128)(2,1)} %refs_2_.1, bf16[1024,256]{1,0:T(8,128)(2,1)} %refs_3_.1, ...), custom_call_target="tpu_custom_call" | custom-call | tf_op jit(solution)/shard_map/forward/pallas_call | solution.py:466
  15.8 0.6 broadcast_in_dim.3.state
  16.5 21.7 %whiten.1 = (f32[16,40,128]{2,1,0:T(8,128)}, f32[136,64]{1,0:T(8,128)}) custom-call(f32[16,40,128]{2,1,0:T(8,128)} %get-tuple-element.23.payload, f32[136,64]{1,0:T(8,128)} %broadcast_in_dim.3.state), custom_call_target="tpu_custom_call" | custom-call | tf_op jit(solution)/shard_map/whiten/pallas_call | solution.py:447
  38.2 9.1 %middle.1 = (f32[784,1024]{1,0:T(8,128)}, bf16[784,1024]{1,0:T(8,128)(2,1)}, bf16[256,1024]{1,0:T(8,128)(2,1)}, f32[256,1024]{1,0:T(8,128)}, f32[8,1024]{1,0:T(8,128)}, /*index=5*/f32[16,40,128]{2,1,0:T(8,128)}) custom-call(f32[16,40,128]{2,1,0:T(8,128)} %get-tuple-element.24.whites.refs_1_, bf16[784,256]{1,0:T(8,128)(2,1)} %get-tuple-element.25.h2.refs_8_, ...), custom_call_target="tpu_custom_call" | custom-call | tf_op jit(solution)/shard_map/middle/pallas_call | solution.py:487
  47.2 23.3 %slope.1 = (f32[16,40,128]{2,1,0:T(8,128)}, f32[136,64]{1,0:T(8,128)}) custom-call(f32[16,40,128]{2,1,0:T(8,128)} %get-tuple-element.26.payload, f32[136,64]{1,0:T(8,128)} %get-tuple-element.27.state), custom_call_target="tpu_custom_call" | custom-call | tf_op jit(solution)/shard_map/slope/pallas_call | solution.py:447
  70.6 14.9 %backward.1 = (bf16[784,1024]{1,0:T(8,128)(2,1)}, f32[256,4480]{1,0:T(8,128)}) custom-call(f32[16,40,128]{2,1,0:T(8,128)} %get-tuple-element.28.refs_0_, f32[16,40,128]{2,1,0:T(8,128)} %get-tuple-element.24.whites.refs_1_, bf16[784,1024]{1,0:T(8,128)(2,1)} %refs_2_.1, bf16[1024,256]{1,0:T(8,128)(2,1)} %refs_3_.1, bf16[2304,256]{1,0:T(8,128)(2,1)} %refs_4_.1, ...), custom_call_target="tpu_custom_call" | custom-call | tf_op jit(solution)/shard_map/backward/pallas_call | solution.py:512
  85.5 0.0 all-reduce.3.cloned.1.call-update
  85.5 275.1 %all-reduce.3.cloned.1.call-done = f32[256,4480]{1,0:T(8,128)} async-done(((f32[256,4480]{1,0:T(8,128)}), f32[256,4480]{1,0:T(8,128)}) %all-reduce.3.cloned.1.call-update) | async-done | bytes 4587536
  360.6 0.9 dynamic-slice_multiply_fusion
  361.5 0.6 slice_reduce_fusion
  362.1 0.6 fusion
  362.7 0.5 slice_bitcast_fusion
Async XLA Ops:
  7.2 353.4 %all-reduce.3.cloned.1.call-start = ((), (), s32[]{:S(2)}) async-start(), calls=%async_computation | async-start | bytes 9175040
Sparse Core Ops, SparseCore 0:
  85.6 274.9 all-reduce.2
where the time goes:
time: 370 us
  waiting for transfers between devices  275 us (74%)
  Pallas kernels  77.6 us (21%)
  between operations  14.1 us (4%)
    unnamed x2, waiting for transfers between devices  275 us
    pallas_call x2, Pallas kernels, exchange(): pl.pallas_call(body, out_shape=(shape((16, 40, 128)), shape((136, 64))),...  45 us
    pallas_call x1, Pallas kernels, backward(): pl.pallas_call(body, out_shape=(shape((rows, 1024), BF16), shape((256, 44...  14.9 us
    pallas_call x1, Pallas kernels, middle(): pl.pallas_call(middle_kernel, out_shape=(shape((rows, 1024)), shape((rows...  9.06 us
    pallas_call x1, Pallas kernels, forward(): pl.pallas_call(forward_kernel, out_shape=(shape((rows, 256), BF16), shape...  8.61 us
  transfers between devices with their start and end apart: 1, of which 1 were waited for; matrix products, arithmetic and copies ran while one was open for 0% of the time, Pallas kernels for 0%

commit v1 on v0

--- a/solution.py
+++ b/solution.py
@@ -253,25 +253,116 @@
         high, low = parts(across[:, here], 2)
         white = parts(diagonal[j], 2)
         value = dot_parts([high], white, ((1,), (1,))) + dot(low, white[0], ((1,), (1,)))
-        last[:, here] = value + dot_parts(grams, [e[:, here]])
+        value = value + dot_parts(grams, [e[:, here]])
+        for half in range(2):
+            last[2 * j + half] = value[:, half * 128 : half * 128 + 128]
     for j in range(8):
         here = slice(j * 128, j * 128 + 128)
-        grads[:, 3328 + j * 128 : 3456 + j * 128] = last[:, here] - hsum[...] * row[0:1, here]
-    for half in range(2):
-        for q in range(4):
-            at = q * 256 + half * 128
-            grads[:, at : at + 128] = top[half, pl.ds(q, 256, stride=4), :]
-        for q in range(9):
-            at = 1024 + q * 256 + half * 128
-            grads[:, at : at + 128] = mid[half, pl.ds(q, 256, stride=9), :]
+        last[j] = last[j] - hsum[...] * row[0:1, here]
+    pack_grads(grads, top, mid, last, gains)
+
+
+SLOTS = 40
+
+
+def slot_rows(core, slot):
+    return pl.ds(core * 128 * SLOTS + slot, 128, stride=SLOTS)
+
+
+def pack_grads(grads, top, mid, last, gains):
+    for core in range(2):
+        for j in range(8):
+            grads[slot_rows(core, j), :] = last[j, pl.ds(core, 128, stride=2), :]
+        for half in range(2):
+            for q in range(9):
+                grads[slot_rows(core, 8 + 2 * q + half), :] = mid[half, pl.ds(q + 9 * core, 128, stride=18), :]
+            for q in range(4):
+                grads[slot_rows(core, 32 + 2 * q + half), :] = top[half, pl.ds(q + 4 * core, 128, stride=8), :]
     total = jnp.sum(gains[...], axis=0, keepdims=True)
-    own = lax.broadcasted_iota(jnp.int32, (256, 1024), 0)
+    row = lax.broadcasted_iota(jnp.int32, (256, 1024), 0)
+    own = (row & 127) * 2 + (row >> 7)
     channel = lax.broadcasted_iota(jnp.int32, (256, 1024), 1)
     spread = jnp.where((channel >> 2) == own, total, 0.0)
     channel = lax.broadcasted_iota(jnp.int32, (1024, 128), 0)
     lane = lax.broadcasted_iota(jnp.int32, (1024, 128), 1)
     pick = jnp.where((channel & 3) == lane, 1.0, 0.0).astype(BF16)
-    grads[:, 4352:4480] = dot_parts(parts(spread, 3), [pick])
+    value = dot_parts(parts(spread, 3), [pick])
+    for core in range(2):
+        grads[slot_rows(core, 26), :] = value[core * 128 : core * 128 + 128]
+        for slot in range(27, 32):
+            grads[slot_rows(core, slot), :] = jnp.zeros((128, 128), F32)
+
+
+def scatter_kernel(scale, grads, out, other, total, wide_a, wide_b, thin_a, thin_b, half_a, half_b, last, sems):
+    z, ghost = lax.axis_index("group"), lax.axis_index("ghost")
+    x, y, core = ghost // 8, (ghost // 2) % 4, ghost % 2
+
+    def device(z, x, y, core):
+        return (z, x * 8 + y * 2 + core)
+
+    partner = device(z, x, y, 1 - core)
+    xs = [device(z, (x + s) % 4, y, core) for s in range(4)]
+    ys = [device(z, x, (y + s) % 4, core) for s in range(4)]
+    zs = [device((z + s) % 8, x, y, core) for s in range(8)]
+    barrier = pltpu.get_barrier_semaphore()
+    for peer in [partner] + xs[1:] + ys[1:] + zs[1:]:
+        pl.semaphore_signal(barrier, inc=1, device_id=peer, device_id_type=MESH)
+    pl.semaphore_wait(barrier, 14)
+    send, recv = sems
+
+    def copy(source, target, at, peer):
+        return pltpu.make_async_remote_copy(
+            src_ref=source, dst_ref=target, send_sem=send.at[at], recv_sem=recv.at[at],
+            device_id=peer, device_id_type=MESH,
+        )
+
+    swaps = [copy(grads.at[1 - core, 4 * h : 4 * h + 4], other.at[4 * h : 4 * h + 4], h, partner) for h in range(2)]
+    for swap in swaps:
+        swap.start()
+    first_a = [copy(total.at[0:4, (x + s) % 4], wide_a.at[s], 4 + s, xs[s]) for s in range(1, 4)]
+    first_b = [copy(total.at[4:8, :, (y + s) % 4], wide_b.at[s], 8 + s, ys[s]) for s in range(1, 4)]
+    for h, group in enumerate((first_a, first_b)):
+        swaps[h].wait_recv()
+
+        def join(i, carry):
+            total[4 * h + i] = grads[core, 4 * h + i] + other[4 * h + i]
+            return carry
+
+        lax.fori_loop(0, 4, join, 0)
+        for one in group:
+            one.start()
+    then_a = [copy(half_a.at[:, (y + s) % 4], thin_a.at[s], 12 + s, ys[s]) for s in range(1, 4)]
+    then_b = [copy(half_b.at[:, (x + s) % 4], thin_b.at[s], 16 + s, xs[s]) for s in range(1, 4)]
+    for one in first_a:
+        one.wait_recv()
+    for i in range(4):
+        half_a[i] = total[i, x] + wide_a[1, i] + wide_a[2, i] + wide_a[3, i]
+    for one in then_a:
+        one.start()
+    for one in first_b:
+        one.wait_recv()
+    for i in range(4):
+        half_b[i] = total[4 + i, :, y] + wide_b[1, i] + wide_b[2, i] + wide_b[3, i]
+    for one in then_b:
+        one.start()
+    final = [copy(other.at[(z + s) % 8, 0, 0], last.at[s], 20 + s, zs[s]) for s in range(1, 8)]
+    for one in then_a:
+        one.wait_recv()
+    for i in range(4):
+        other[i, 0, 0] = half_a[i, y] + thin_a[1, i] + thin_a[2, i] + thin_a[3, i]
+    for one in then_b:
+        one.wait_recv()
+    for i in range(4):
+        other[4 + i, 0, 0] = half_b[i, x] + thin_b[1, i] + thin_b[2, i] + thin_b[3, i]
+    for one in final:
+        one.start()
+    result = other[z, 0, 0]
+    for s in range(1, 8):
+        final[s - 1].wait_recv()
+        result = result + last[s]
+    out[...] = result * scale
+    for one in swaps + first_a + first_b + then_a + then_b + final:
+        one.wait_send()
 
 
 def newton(n, size):
@@ -511,7 +602,7 @@
 
     return pl.pallas_call(
         body,
-        out_shape=(shape((rows, 1024), BF16), shape((256, 4480))),
+        out_shape=(shape((rows, 1024), BF16), shape((256 * SLOTS, 128))),
         in_specs=[VM] * len(args),
         out_specs=[VM] * 2,
         scratch_shapes=[
@@ -520,7 +611,7 @@
             pltpu.VMEM((rows, 2304), BF16),
             pltpu.VMEM((4, 256, 256), F32),
             pltpu.VMEM((256, 1024), BF16),
-            pltpu.VMEM((256, 1024), F32),
+            pltpu.VMEM((8, 256, 128), F32),
             pltpu.VMEM((2, 2304, 128), F32),
             pltpu.VMEM((2, 1024, 128), F32),
             pltpu.VMEM((8, 1024), F32),
@@ -528,6 +619,37 @@
         compiler_params=LIMIT,
         name="backward",
     )(*args)
+
+
+def scatter(grads, scale):
+    def body(grads, out, other, total, wide_a, wide_b, thin_a, thin_b, half_a, half_b, last, *sems):
+        scatter_kernel(
+            scale, grads, out, other, total, wide_a, wide_b, thin_a, thin_b, half_a, half_b, last, sems
+        )
+
+    dma = pltpu.SemaphoreType.DMA
+    return pl.pallas_call(
+        body,
+        out_shape=shape((SLOTS, 128)),
+        in_specs=[VM],
+        out_specs=VM,
+        scratch_shapes=[
+            pltpu.VMEM((8, 4, 4, SLOTS, 128), F32),
+            pltpu.VMEM((8, 4, 4, SLOTS, 128), F32),
+            pltpu.VMEM((4, 4, 4, SLOTS, 128), F32),
+            pltpu.VMEM((4, 4, 4, SLOTS, 128), F32),
+            pltpu.VMEM((4, 4, SLOTS, 128), F32),
+            pltpu.VMEM((4, 4, SLOTS, 128), F32),
+            pltpu.VMEM((4, 4, SLOTS, 128), F32),
+            pltpu.VMEM((4, 4, SLOTS, 128), F32),
+            pltpu.VMEM((8, SLOTS, 128), F32),
+            dma((28,)), dma((28,)),
+        ],
+        compiler_params=pltpu.CompilerParams(
+            collective_id=2, has_side_effects=True, vmem_limit_bytes=60 * 1024 * 1024
+        ),
+        name="scatter",
+    )(grads)
 
 
 def shards(inputs, out_grad, conv_first, conv_middle, conv_last, gain):
@@ -543,9 +665,10 @@
         span, slopes, whites, inputs, conv_first, conv_middle, conv_last, h1, s1, h2, s2, gram, hsum,
         dpre, dwhite, d, across, gains,
     )
-    grads = lax.psum_scatter(grads, ("group", "ghost"), scatter_dimension=0, tiled=True)
-    grads = grads.reshape(-1) * (span * groups) ** (-0.5)
-    return input_grad, grads[:1024], grads[1024:3328], grads[3328:4352], grads[4352:4356]
+    sums = scatter(grads.reshape(2, 8, 4, 4, SLOTS, 128), (span * groups) ** (-0.5))
+    return (
+        input_grad, sums[32:40].reshape(-1), sums[8:26].reshape(-1), sums[0:8].reshape(-1), sums[26, :4]
+    )
 
 
 def solution(mesh):

time: 370 us -> 130 us (0.35)
  waiting for transfers between devices: 275 us -> 0 us
  Pallas kernels: 77.6 us -> 124 us
  between operations: 14.1 us -> 0.66 us
    unnamed x2 -> x0, waiting for transfers between devices: 275 us -> none
    pallas_call x1 -> x2, Pallas kernels: 14.9 us -> 60.9 us  [the longest x1 44.9 us: scatter(): pl.pallas_call(body, out_shape=shape((SLOTS, 128)), in_specs=[VM], out_sp...]
  transfers between devices with their start and end apart: 1 -> 0, of which waited for: 1 -> 0; matrix products, arithmetic and copies ran while one was open for 0% -> 0% of each run, Pallas kernels for 0% -> 0%
where the time goes in v1:
time: 130 us; the launch traced here: 129 us
  Pallas kernels  124 us (95%)
  local copies, waits for them, and re-layouts  4.4 us (3%)
    pallas_call x2, Pallas kernels, exchange(): pl.pallas_call(body, out_shape=(shape((16, 40, 128)), shape((136, 64))),...  45 us
    pallas_call x1, Pallas kernels, scatter(): pl.pallas_call(body, out_shape=shape((SLOTS, 128)), in_specs=[VM], out_sp...  44.9 us
    pallas_call x1, Pallas kernels, backward(): pl.pallas_call(body, out_shape=(shape((rows, 1024), BF16), shape((256 * S...  16.1 us
    pallas_call x1, Pallas kernels, middle(): pl.pallas_call(middle_kernel, out_shape=(shape((rows, 1024)), shape((rows...  9.06 us
    pallas_call x1, Pallas kernels, forward(): pl.pallas_call(forward_kernel, out_shape=(shape((rows, 256), BF16), shape...  8.61 us

profile of v1, /device:TPU:2, one launch (start us, length us, event | category | flops | bytes accessed | tf_op | source)
XLA Modules:
  0.0 128.7 jit_solution(8761147267728793537)
XLA Ops:
  0.6 8.6 %forward.1 = (bf16[784,256]{1,0:T(8,128)(2,1)}, f32[784,256]{1,0:T(8,128)}, bf16[784,256]{1,0:T(8,128)(2,1)}, f32[784,256]{1,0:T(8,128)}, f32[256,256]{1,0:T(8,1...) custom-call(bf16[784,1024]{1,0:T(8,128)(2,1)} %refs_2_.1, bf16[1024,256]{1,0:T(8,128)(2,1)} %refs_3_.1, ...), custom_call_target="tpu_custom_call" | custom-call | tf_op jit(solution)/shard_map/forward/pallas_call | solution.py:557
  9.2 0.6 broadcast_in_dim.3.state
  9.9 21.7 %whiten.1 = (f32[16,40,128]{2,1,0:T(8,128)}, f32[136,64]{1,0:T(8,128)}) custom-call(f32[16,40,128]{2,1,0:T(8,128)} %get-tuple-element.23.payload, f32[136,64]{1,0:T(8,128)} %broadcast_in_dim.3.state), custom_call_target="tpu_custom_call" | custom-call | tf_op jit(solution)/shard_map/whiten/pallas_call | solution.py:538
  31.6 9.1 %middle.1 = (f32[784,1024]{1,0:T(8,128)}, bf16[784,1024]{1,0:T(8,128)(2,1)}, bf16[256,1024]{1,0:T(8,128)(2,1)}, f32[256,1024]{1,0:T(8,128)}, f32[8,1024]{1,0:T(8,128)}, /*index=5*/f32[16,40,128]{2,1,0:T(8,128)}) custom-call(f32[16,40,128]{2,1,0:T(8,128)} %get-tuple-element.24.whites.refs_1_, bf16[784,256]{1,0:T(8,128)(2,1)} %get-tuple-element.25.h2.refs_8_, ...), custom_call_target="tpu_custom_call" | custom-call | tf_op jit(solution)/shard_map/middle/pallas_call | solution.py:578
  40.7 23.3 %slope.1 = (f32[16,40,128]{2,1,0:T(8,128)}, f32[136,64]{1,0:T(8,128)}) custom-call(f32[16,40,128]{2,1,0:T(8,128)} %get-tuple-element.26.payload, f32[136,64]{1,0:T(8,128)} %get-tuple-element.27.state), custom_call_target="tpu_custom_call" | custom-call | tf_op jit(solution)/shard_map/slope/pallas_call | solution.py:538
  64.0 16.1 %backward.1 = (bf16[784,1024]{1,0:T(8,128)(2,1)}, f32[10240,128]{1,0:T(8,128)}) custom-call(f32[16,40,128]{2,1,0:T(8,128)} %get-tuple-element.28.refs_0_, f32[16,40,128]{2,1,0:T(8,128)} %get-tuple-element.24.whites.refs_1_, bf16[784,1024]{1,0:T(8,128)(2,1)} %refs_2_.1, bf16[1024,256]{1,0:T(8,128)(2,1)} %refs_3_.1, bf16[2304,256]{1,0:T(8,128)(2,1)} %refs_4_.1, ...), custom_call_target="tpu_custom_call" | custom-call | tf_op jit(solution)/shard_map/backward/pallas_call | solution.py:603
  80.0 44.9 %scatter.1 = f32[40,128]{1,0:T(8,128)} custom-call(f32[2,8,4,4,40,128]{5,4,3,2,1,0:T(8,128)} %bitcast.10), custom_call_target="tpu_custom_call" | custom-call | tf_op jit(solution)/shard_map/scatter/pallas_call | solution.py:631
  124.9 1.2 slice_bitcast_fusion.3
  126.1 1.3 slice_bitcast_fusion.1
  127.4 1.3 %slice_bitcast_fusion = f32[2304]{0:T(1024)} fusion(f32[40,128]{1,0:T(8,128)} %scatter.1), kind=kLoop, calls=%fused_computation | loop fusion | bytes 18432 | tf_op jit(solution)/shard_map/reshape | solution.py:670
